TPU v7x, 32 devices: a whole 2x2x4 slice. The times are simulated.
32 devices in a mesh: wide: 16 (over z, x, core), narrow: 2 (over y).
Axes of the slice: x: 2, y: 2, z: 4, core: 2. Of those that a mesh axis runs over, the one named last changes fastest.
Arguments:
- amplitudes: float32 [48, 1024, 1024], P('wide', None, 'narrow'), may hold values from -24 to 24
- integrals: float32 [16, 16, 1024, 1024], P('narrow', None, 'wide'), may hold values from -0.005859375 to 0.005859375
- pair_index: int32 [48, 2], P('wide'), may hold values from 0 to 199
- window_virtuals: int32 [16], replicated, may hold values from 0 to 1023
- occ_energy: float32 [200], replicated, may hold values from -3 to -0.5
- virt_energy: float32 [1024], replicated, may hold values from 0.3 to 6
Outputs:
- update: float32 [16, 16, 48], P('narrow', None, 'wide')
All inputs are finite; a program needn't handle non-finite values.
Results may differ from a plain program's by a relative error of at most 0.00013.
Values sent between devices are 32-bit elements; how exact they have to be, the bound alone decides.
No kernel may reach another device: no remote copies, remote signals or barrier semaphores. Data moves between devices by JAX's collectives and lax.ppermute only.
A program may use at most 128 MiB of HBM per device.

v0:
```python
import jax
import jax.numpy as jnp
from jax import lax
from jax.sharding import PartitionSpec as P


def lookup(table, indices):
    matches = (indices[..., None] == jnp.arange(table.shape[0], dtype=jnp.int32)).astype(
        jnp.float32
    )
    return jnp.sum(matches * table, axis=-1)


def contract(left_rows, right_rows):
    return lax.dot_general(
        left_rows.reshape(left_rows.shape[0], -1),
        right_rows.reshape(right_rows.shape[0], -1),
        (((1,), (1,)), ((), ())),
        precision=lax.Precision.HIGHEST,
        preferred_element_type=jnp.float32,
    )


def shards(amplitudes, integrals, pair_index, window_virtuals, occ_energy, virt_energy):
    exchanged = lax.all_to_all(amplitudes, "wide", split_axis=1, concat_axis=0, tiled=True)
    rows_here = integrals.shape[0]
    window = integrals.shape[1]
    first_block = integrals.shape[2]
    all_pairs = exchanged.shape[0]
    integral_rows = integrals.reshape(rows_here * window, first_block, integrals.shape[3])
    partial_value = contract(integral_rows, lax.all_gather(exchanged, "narrow", axis=2, tiled=True))
    ladder = lax.psum_scatter(
        partial_value.reshape(rows_here, window, all_pairs), "wide", scatter_dimension=2, tiled=True
    )
    swapped = lax.all_to_all(ladder, "narrow", split_axis=1, concat_axis=0, tiled=True)
    combined = ladder + jnp.transpose(swapped, (1, 0, 2))
    row_start = lax.axis_index("narrow") * rows_here
    own_virtuals = lax.dynamic_slice_in_dim(window_virtuals, row_start, rows_here, 0)
    row_energy = lookup(virt_energy, own_virtuals)
    column_energy = lookup(virt_energy, window_virtuals)
    pair_energy = lookup(occ_energy, pair_index[:, 0]) + lookup(occ_energy, pair_index[:, 1])
    denominator = (
        pair_energy[None, None, :] - row_energy[:, None, None] - column_energy[None, :, None]
    )
    return combined / denominator


def solution(mesh):
    in_specs = (
        P("wide", None, "narrow"),
        P("narrow", None, "wide", None),
        P("wide", None),
        P(),
        P(),
        P(),
    )
    out_specs = P("narrow", None, "wide")
    return jax.shard_map(shards, mesh=mesh, in_specs=in_specs, out_specs=out_specs, check_vma=False)
```

profile of v0, /device:TPU:0, one launch (start us, length us, event | category | flops | bytes accessed | tf_op | source)
XLA Modules:
  0.0 489.2 jit_solution(3291001078130395045)
XLA Ops:
  6.5 0.0 all-gather.2.cloned.1.call-start
  6.5 7.1 %copy.42 = f32[3,1024,512]{2,0,1:T(4,128)S(1)} copy(f32[3,1024,512]{2,1,0:T(8,128)} %param.6) | data formatting | bytes 12582912 | tf_op args[0]
  13.6 189.3 %all_to_all.36 = f32[3,1024,512]{2,0,1:T(4,128)S(1)} all-to-all(f32[3,1024,512]{2,0,1:T(4,128)S(1)} %copy.42), channel_id=1, replica_groups=mesh['wide'=16,'narrow'=2] {'wide'}, dimensions={1} | all-to-all | bytes 12582912 | tf_op jit(solution)/shard_map/all_to_all | solution.py:25
  202.9 2.0 copy.43
  205.0 1.2 copy.44
  206.2 0.0 copy-start.3
  206.2 0.0 copy-start.2
  206.2 0.0 copy-start.1
  206.2 0.0 copy-start
  206.3 6.3 %copy.45 = f32[48,64,512]{2,0,1:T(8,128)} copy(f32[48,64,512]{2,1,0:T(8,128)S(1)} %bitcast.30) | data formatting | bytes 12582912 | tf_op jit(solution)/shard_map/all_to_all | solution.py:25
  212.5 0.0 all-gather.2.cloned.1.call-update
  212.5 0.0 reduce-scatter.4.cloned.1.call-start
  212.6 0.0 copy-done.3
  212.6 0.1 dynamic_slice.3
  212.7 0.0 copy-done.2
  212.7 0.0 copy-done.1
  212.7 0.2 select_reduce_fusion.2
  212.9 0.0 copy-done
  212.9 0.2 select_reduce_fusion.1
  213.1 153.1 %all-gather.2.cloned.1.call-done = f32[48,64,1024]{2,0,1:T(8,128)} async-done(((f32[48,64,512]{2,0,1:T(8,128)}), f32[48,64,1024]{2,0,1:T(8,128)}) %all-gather.2.cloned.1.call-update) | async-done | bytes 12582928 | tf_op jit(solution)/shard_map/all_gather | solution.py:31
  366.2 50.3 %fusion.3 = f32[8,16,48]{2,1,0:T(8,128)S(1)} fusion(f32[48,64,1024]{2,0,1:T(8,128)} %all-gather.2.cloned.1.call-done, f32[8,16,64,1024]{3,2,1,0:T(8,128)} %param.7), kind=kOutput, calls=%fused_computation.3 | convolution fusion | flops 4831838208 | bytes 46161920 | tf_op jit(solution)/shard_map/dot_general | solution.py:15
  416.6 0.8 copy.47
  417.4 0.0 reduce-scatter.4.cloned.1.call-update
  417.4 0.1 broadcast_subtract_fusion
  417.5 53.7 %reduce-scatter.4.cloned.1.call-done = f32[8,16,3]{1,0,2:T(8,128)} async-done(((f32[8,16,48]{1,0,2:T(8,128)}), f32[8,16,3]{1,0,2:T(8,128)}) %reduce-scatter.4.cloned.1.call-update) | async-done | bytes 1552
  471.2 0.8 copy.48
  471.9 0.7 reshape.46
  472.6 3.2 all-to-all-start.1
  475.8 0.2 select_reduce_fusion
  476.0 3.6 all-to-all-done.1
  479.6 0.5 broadcast.40
  480.1 0.7 reduce
  480.8 0.1 reshape.47
  480.9 0.1 all_to_all.33
  481.0 1.4 fusion.8
  (3 shorter events, 0.0 us)
Async XLA Ops:
  6.5 359.7 %all-gather.2.cloned.1.call-start = ((), (), s32[]{:S(2)}) async-start(), calls=%async_computation.3 | async-start | bytes 18874368 | tf_op jit(solution)/shard_map/all_gather | solution.py:31
  206.2 6.4 %copy-start.3 = (s32[16]{0:T(128)S(1)}, s32[16]{0:T(128)}, u32[]{:S(2)}) copy-start(s32[16]{0:T(128)} %param.9) | copy-start | bytes 196
  206.2 6.5 %copy-start.2 = (s32[3,2]{0,1:T(2,128)S(1)}, s32[3,2]{0,1:T(2,128)}, u32[]{:S(2)}) copy-start(s32[3,2]{0,1:T(2,128)} %param.8) | copy-start | bytes 76
  206.2 6.5 %copy-start.1 = (f32[200]{0:T(256)S(1)}, f32[200]{0:T(256)}, u32[]{:S(2)}) copy-start(f32[200]{0:T(256)} %param.10) | copy-start | bytes 2404
  206.2 6.7 %copy-start = (f32[1024]{0:T(1024)S(1)}, f32[1024]{0:T(1024)}, u32[]{:S(2)}) copy-start(f32[1024]{0:T(1024)} %param.11) | copy-start | bytes 12292
  212.5 258.6 %reduce-scatter.4.cloned.1.call-start = ((), (), s32[]{:S(2)}) async-start(), calls=%async_computation.4 | async-start | bytes 208896
  472.6 7.0 %all-to-all-start.1 = ((f32[2,1,192]{2,1,0:T(1,128)}), f32[2,1,192]{2,1,0:T(1,128)S(1)}, u32[]{:S(2)}, u32[]{:S(2)}) async-start(f32[2,1,192]{2,1,0:T(1,128)} %reshape.46), calls=%async_computation.1 | async-start | bytes 4096 | tf_op jit(solution)/shard_map/all_to_all | solution.py:35
Sparse Core Ops, SparseCore 0:
  212.7 153.5 all-gather.1
  417.5 53.5 reduce-scatter.3
where the time goes:
time: 490 us; the launch traced here: 489 us
  waiting for transfers between devices  210 us (43%)
  blocking collectives  189 us (39%)
  matrix products  50.3 us (10%)
  local copies, waits for them, and re-layouts  19.7 us (4%)
  between operations  13.5 us (3%)
    all_to_all x1, blocking collectives, shards(): lax.all_to_all(amplitudes, 'wide', split_axis=1, concat_axis=0, tiled=True)  189 us
    all_gather x1, waiting for transfers between devices, shards(): lax.all_gather(exchanged, 'narrow', axis=2, tiled=True)  153 us
    unnamed x3, waiting for transfers between devices  53.7 us
    dot_general x1, matrix products, contract(): lax.dot_general(left_rows.reshape(left_rows.shape[0], -1), right_rows.res...  50.3 us
  transfers between devices with their start and end apart: 3, of which 3 were waited for; matrix products, arithmetic and copies ran while one was open for 0% of the time, Pallas kernels for 0%

commit v1 on v0

--- a/solution.py
+++ b/solution.py
@@ -22,7 +22,12 @@
 
 
 def shards(amplitudes, integrals, pair_index, window_virtuals, occ_energy, virt_energy):
-    exchanged = lax.all_to_all(amplitudes, "wide", split_axis=1, concat_axis=0, tiled=True)
+    exchanged = jnp.concatenate(
+        lax.all_to_all(
+            jnp.stack(jnp.split(amplitudes, lax.axis_size("wide"), axis=1)), "wide", 0, 0
+        ),
+        axis=0,
+    )
     rows_here = integrals.shape[0]
     window = integrals.shape[1]
     first_block = integrals.shape[2]

time: 490 us -> 451 us (0.920)
  local copies, waits for them, and re-layouts: 19.7 us -> 69.2 us
  blocking collectives: 189 us -> 144 us
  waiting for transfers between devices: 210 us -> 177 us
  matrix products: 50.3 us -> 39.2 us
    unnamed x11 -> x27, local copies, waits for them, and re-layouts: 7.9 us -> 65.9 us
    all_to_all x1, blocking collectives: 189 us -> 144 us  [shards(): lax.all_to_all(jnp.stack(jnp.split(amplitudes, lax.axis_size('wide'), axi...]
    all_gather x1, waiting for transfers between devices: 153 us -> 120 us  [shards(): lax.all_gather(exchanged, 'narrow', axis=2, tiled=True)]
    dot_general x1, matrix products: 50.3 us -> 39.2 us  [contract(): lax.dot_general(left_rows.reshape(left_rows.shape[0], -1), right_rows.res...]
    all_to_all x3 -> x0, local copies, waits for them, and re-layouts: 9.52 us -> none  [shards(): lax.all_to_all(amplitudes, 'wide', split_axis=1, concat_axis=0, tiled=True)]
  transfers between devices with their start and end apart: 3 -> 3, of which waited for: 3 -> 3; matrix products, arithmetic and copies ran while one was open for 0% -> 8% of each run, Pallas kernels for 0% -> 0%
where the time goes in v1:
time: 451 us; the launch traced here: 449 us
  waiting for transfers between devices  177 us (39%)
  blocking collectives  144 us (32%)
  local copies, waits for them, and re-layouts  69.2 us (15%)
  matrix products  39.2 us (9%)
  between operations  13.6 us (3%)
    all_to_all x1, blocking collectives, shards(): lax.all_to_all(jnp.stack(jnp.split(amplitudes, lax.axis_size('wide'), axi...  144 us
    all_gather x1, waiting for transfers between devices, shards(): lax.all_gather(exchanged, 'narrow', axis=2, tiled=True)  120 us
    unnamed x27, local copies, waits for them, and re-layouts  65.9 us
    unnamed x3, waiting for transfers between devices  53.7 us
    dot_general x1, matrix products, contract(): lax.dot_general(left_rows.reshape(left_rows.shape[0], -1), right_rows.res...  39.2 us
  transfers between devices with their start and end apart: 3, of which 3 were waited for; matrix products, arithmetic and copies ran while one was open for 8% of the time, Pallas kernels for 0%

profile of v1, /device:TPU:0, one launch (start us, length us, event | category | flops | bytes accessed | tf_op | source)
XLA Modules:
  0.0 449.4 jit_solution(14589296256108769780)
XLA Ops:
  6.5 0.0 all-gather.2.cloned.1.call-start
  6.5 1.0 bitcast_dynamic-update-slice_fusion.15
  7.6 1.0 bitcast_dynamic-update-slice_fusion.14
  8.6 1.0 bitcast_dynamic-update-slice_fusion.13
  9.6 1.0 bitcast_dynamic-update-slice_fusion.12
  10.7 1.0 bitcast_dynamic-update-slice_fusion.11
  11.7 1.0 bitcast_dynamic-update-slice_fusion.10
  12.7 1.0 bitcast_dynamic-update-slice_fusion.9
  13.8 1.0 bitcast_dynamic-update-slice_fusion.8
  14.8 1.0 bitcast_dynamic-update-slice_fusion.7
  15.8 1.0 bitcast_dynamic-update-slice_fusion.6
  16.9 1.0 bitcast_dynamic-update-slice_fusion.5
  17.9 1.0 bitcast_dynamic-update-slice_fusion.4
  18.9 1.0 bitcast_dynamic-update-slice_fusion.3
  20.0 1.0 bitcast_dynamic-update-slice_fusion.2
  21.0 1.0 bitcast_dynamic-update-slice_fusion.1
  22.0 1.0 bitcast_dynamic-update-slice_fusion
  23.1 144.5 %all_to_all.23 = f32[16,3,64,512]{3,2,1,0:T(8,128)} all-to-all(f32[16,3,64,512]{3,2,1,0:T(8,128)S(1)} %bitcast_dynamic-update-slice_fusion), channel_id=1, replica_groups=mesh['wide'=16,'narrow'=2] {'wide'}, dimensions={0} | all-to-all | bytes 12582912 | tf_op jit(solution)/shard_map/all_to_all | solution.py:26
  167.5 0.0 all-gather.2.cloned.1.call-update
  167.6 0.0 reduce-scatter.4.cloned.1.call-start
  167.6 0.0 copy-start.3
  167.6 0.0 copy-start.2
  167.6 0.0 copy-start.1
  167.6 0.0 copy-start
  167.7 33.2 %copy.20 = f32[16,8,64,1024]{3,1,2,0:T(8,128)} copy(f32[16,8,64,1024]{3,2,1,0:T(8,128)} %bitcast.62) | data formatting | bytes 67108864
  200.8 0.0 copy-done.3
  200.8 0.1 dynamic_slice.3
  200.9 0.0 copy-done.2
  200.9 0.0 copy-done.1
  200.9 0.2 select_reduce_fusion.2
  201.1 0.0 copy-done
  201.2 0.2 select_reduce_fusion.1
  201.3 119.7 %all-gather.2.cloned.1.call-done = f32[48,64,1024]{2,1,0:T(8,128)} async-done(((f32[48,64,512]{2,1,0:T(8,128)}), f32[48,64,1024]{2,1,0:T(8,128)}) %all-gather.2.cloned.1.call-update) | async-done | bytes 12582928 | tf_op jit(solution)/shard_map/all_gather | solution.py:36
  321.1 16.4 %copy.19 = f32[6,8,64,1024]{3,1,2,0:T(8,128)} copy(f32[6,8,64,1024]{3,2,1,0:T(8,128)} %bitcast.64) | data formatting | bytes 25165824
  337.5 39.2 %convolution_bitcast_fusion = f32[128,48]{0,1:T(8,128)S(1)} fusion(f32[48,65536]{1,0:T(8,128)} %bitcast.61, f32[128,65536]{1,0:T(8,128)} %bitcast.60), kind=kOutput, calls=%fused_computation | convolution fusion | flops 4831838208 | bytes 46161920 | tf_op jit(solution)/shard_map/dot_general | solution.py:15
  376.7 0.1 copy.15
  376.8 0.8 copy.16
  377.6 0.0 reduce-scatter.4.cloned.1.call-update
  377.6 0.1 broadcast_subtract_fusion
  377.7 53.7 %reduce-scatter.4.cloned.1.call-done = f32[8,16,3]{1,0,2:T(8,128)} async-done(((f32[8,16,48]{1,0,2:T(8,128)}), f32[8,16,3]{1,0,2:T(8,128)}) %reduce-scatter.4.cloned.1.call-update) | async-done | bytes 1552
  431.3 0.8 copy.17
  432.1 0.7 reshape.52
  432.8 3.2 all-to-all-start.1
  436.0 0.2 select_reduce_fusion
  436.2 3.6 all-to-all-done.1
  439.8 0.5 broadcast.40
  440.3 0.7 reduce
  441.0 0.1 reshape.53
  441.1 0.1 all_to_all.20
  441.2 1.4 fusion
  (3 shorter events, 0.0 us)
Async XLA Ops:
  6.5 314.5 %all-gather.2.cloned.1.call-start = ((), (), s32[]{:S(2)}) async-start(), calls=%async_computation.3 | async-start | bytes 18874368 | tf_op jit(solution)/shard_map/all_gather | solution.py:36
  167.6 263.8 %reduce-scatter.4.cloned.1.call-start = ((), (), s32[]{:S(2)}) async-start(), calls=%async_computation.4 | async-start | bytes 208896
  167.6 33.2 %copy-start.3 = (s32[16]{0:T(128)S(1)}, s32[16]{0:T(128)}, u32[]{:S(2)}) copy-start(s32[16]{0:T(128)} %param.9) | copy-start | bytes 196
  167.6 33.3 %copy-start.2 = (s32[3,2]{0,1:T(2,128)S(1)}, s32[3,2]{0,1:T(2,128)}, u32[]{:S(2)}) copy-start(s32[3,2]{0,1:T(2,128)} %param.8) | copy-start | bytes 76
  167.6 33.3 %copy-start.1 = (f32[200]{0:T(256)S(1)}, f32[200]{0:T(256)}, u32[]{:S(2)}) copy-start(f32[200]{0:T(256)} %param.10) | copy-start | bytes 2404
  167.6 33.5 %copy-start = (f32[1024]{0:T(1024)S(1)}, f32[1024]{0:T(1024)}, u32[]{:S(2)}) copy-start(f32[1024]{0:T(1024)} %param.11) | copy-start | bytes 12292
  432.8 7.0 %all-to-all-start.1 = ((f32[2,1,192]{2,1,0:T(1,128)}), f32[2,1,192]{2,1,0:T(1,128)S(1)}, u32[]{:S(2)}, u32[]{:S(2)}) async-start(f32[2,1,192]{2,1,0:T(1,128)} %reshape.52), calls=%async_computation.1 | async-start | bytes 4096 | tf_op jit(solution)/shard_map/all_to_all | solution.py:40
Sparse Core Ops, SparseCore 0:
  167.7 153.3 all-gather.1
  377.7 53.5 reduce-scatter.3
